TPU v7x, 32 devices: a whole 2x2x4 slice. The times are simulated.
32 devices in a mesh: dp: 8 (over y, x, core), mp: 4 (over z).
Axes of the slice: x: 2, y: 2, z: 4, core: 2. Of those that a mesh axis runs over, the one named last changes fastest.
Arguments:
- latents: float32 [3, 8192, 1024], P(None, ('dp', 'mp')), may hold values from -6 to 6
- group_ids: int32 [3, 8, 1024], P(None, 'dp'), may hold values from 0 to 15, never falling along the last dimension, each value on 1 to 128 neighbouring positions
- pad_mask: int32 [3, 8, 1024], P(None, 'dp'), may hold values 0 or 1
- w_qkv: bfloat16 [3, 1024, 1024], P(None, 'dp', 'mp'), may hold values from -0.1875 to 0.1875
- w_out: bfloat16 [1024, 1024], P('dp', 'mp'), may hold values from -0.5 to 0.5
- w_up: bfloat16 [1024, 4096], P('dp', 'mp'), may hold values from -0.1875 to 0.1875
- w_down: bfloat16 [1024, 4096], P('dp', 'mp'), may hold values from -0.09375 to 0.09375
- norm_gain: bfloat16 [2, 1024], P(None, 'dp'), may hold values from 0.099609375 to 1.8984375
- norm_bias: bfloat16 [2, 1024], P(None, 'dp'), may hold values from -3 to 3
- out_grad: float32 [3, 8192, 1024], P(None, ('dp', 'mp')), may hold values from -6 to 6
Outputs:
- latents_out: float32 [3, 8192, 1024], P(None, ('dp', 'mp'))
- latents_grad: float32 [3, 8192, 1024], P(None, ('dp', 'mp'))
- grad_qkv: float32 [3, 1024, 1024], P(None, 'dp', 'mp')
- grad_out: float32 [1024, 1024], P('dp', 'mp')
- grad_up: float32 [1024, 4096], P('dp', 'mp')
- grad_down: float32 [1024, 4096], P('dp', 'mp')
- grad_gain: float32 [2, 1024], P(None, 'dp')
- grad_bias: float32 [2, 1024], P(None, 'dp')
Inputs may be any that keep to these rules, and one draw needn't show every extreme that they name: `group_ids`: group numbers along one clip never fall; each group of a clip holds 1 to 128 latents and one holds exactly 128.
All inputs are finite; a program needn't handle non-finite values. No bound on the sum of `pad_mask` on one device may be relied on, other than what follows from the above.
Results may differ from a plain program's by a relative error of at most 0.0095.
Values may be sent and summed in bfloat16 or wider, within the bound.
No kernel may reach another device: no remote copies, remote signals or barrier semaphores. Data moves between devices by JAX's collectives and lax.ppermute only.
A program may use at most 192 MiB of HBM per device.

v0:
```python
import jax
import jax.numpy as jnp
from jax import lax
from jax.sharding import PartitionSpec as P

HEAD_DIM = 128
epsilon = 1e-05


def norm_rows(values, scaling, offset):
    row_mean = jnp.mean(values, axis=-1, keepdims=True)
    centred = values - row_mean
    row_var = jnp.mean(centred * centred, axis=-1, keepdims=True)
    return centred * lax.rsqrt(row_var + epsilon) * scaling + offset


def spread_rows(rows_local):
    return lax.all_gather(rows_local, "mp", axis=0, tiled=True)


def settle_rows(partial_rows):
    return lax.psum_scatter(partial_rows, "mp", scatter_dimension=0, tiled=True)


def block_mask(group_row, live_row, first_row, block_rows):
    positions = jnp.arange(group_row.shape[0], dtype=jnp.int32)
    query_positions = first_row + jnp.arange(block_rows, dtype=jnp.int32)
    query_groups = lax.dynamic_slice_in_dim(group_row, first_row, block_rows)
    same_group = query_groups[:, None] == group_row[None, :]
    return same_group & (
        (live_row[None, :] == 1) | (query_positions[:, None] == positions[None, :])
    )


def block_scores(query_block, keys, allowed, factor):
    scores = (
        jnp.einsum("qhd,khd->hqk", query_block, keys, preferred_element_type=jnp.float32) * factor
    )
    return jnp.where(allowed[None], scores, -1e30)


def attend_forward(queries, keys, values, group_row, live_row, block_rows, factor):
    seq_len = keys.shape[0]
    block_count = seq_len // block_rows

    def one_block(block_index):
        first_row = block_index * block_rows
        query_block = lax.dynamic_slice_in_dim(queries, first_row, block_rows, 0)
        scores = block_scores(
            query_block, keys, block_mask(group_row, live_row, first_row, block_rows), factor
        )
        row_peak = jnp.max(scores, axis=-1, keepdims=True)
        weights = jnp.exp(scores - row_peak)
        totals = jnp.sum(weights, axis=-1, keepdims=True)
        probabilities = (weights / totals).astype(jnp.bfloat16)
        mixture = jnp.einsum(
            "hqk,khd->qhd", probabilities, values, preferred_element_type=jnp.float32
        )
        return (mixture, (row_peak + jnp.log(totals))[..., 0])

    mixture, log_totals = lax.map(one_block, jnp.arange(block_count, dtype=jnp.int32))
    return (mixture.reshape(seq_len, mixture.shape[2], mixture.shape[3]), log_totals)


def attend_backward(
    queries, keys, values, grad_mix, log_totals, group_row, live_row, block_rows, factor
):
    seq_len = keys.shape[0]
    block_count = seq_len // block_rows

    def one_block(carry, block_index):
        grad_keys, grad_values = carry
        first_row = block_index * block_rows
        query_block = lax.dynamic_slice_in_dim(queries, first_row, block_rows, 0)
        grad_block = lax.dynamic_slice_in_dim(grad_mix, first_row, block_rows, 0)
        scores = block_scores(
            query_block, keys, block_mask(group_row, live_row, first_row, block_rows), factor
        )
        probabilities = jnp.exp(scores - log_totals[block_index][:, :, None])
        grad_probs = jnp.einsum(
            "qhd,khd->hqk", grad_block, values, preferred_element_type=jnp.float32
        )
        weighted = jnp.sum(probabilities * grad_probs, axis=-1, keepdims=True)
        grad_scores = (probabilities * (grad_probs - weighted)).astype(jnp.bfloat16)
        grad_query = (
            jnp.einsum("hqk,khd->qhd", grad_scores, keys, preferred_element_type=jnp.float32)
            * factor
        )
        grad_keys = (
            grad_keys
            + jnp.einsum(
                "hqk,qhd->khd", grad_scores, query_block, preferred_element_type=jnp.float32
            )
            * factor
        )
        grad_values = grad_values + jnp.einsum(
            "hqk,qhd->khd",
            probabilities.astype(jnp.bfloat16),
            grad_block,
            preferred_element_type=jnp.float32,
        )
        return ((grad_keys, grad_values), grad_query)

    zeros_kv = jnp.zeros(keys.shape, jnp.float32)
    (grad_keys, grad_values), grad_query = lax.scan(
        one_block, (zeros_kv, zeros_kv), jnp.arange(block_count, dtype=jnp.int32)
    )
    return (grad_query.reshape(keys.shape), grad_keys, grad_values)


def forward_pass(latent_rows, weights, groups, masks, block_rows, factor):
    qkv_rows, out_rows, up_rows, down_rows, gains, offsets = weights
    gains_full = gains.astype(jnp.float32)
    offsets_full = offsets.astype(jnp.float32)
    seq_count = groups.shape[0]
    seq_len = groups.shape[1]
    inputs_a = spread_rows(
        norm_rows(latent_rows, gains_full[0], offsets_full[0]).astype(jnp.bfloat16)
    )
    projected = jnp.einsum(
        "rd,tde->tre", inputs_a, qkv_rows, preferred_element_type=jnp.float32
    ).astype(jnp.bfloat16)
    local_heads = projected.shape[2] // HEAD_DIM
    shaped = projected.reshape(3, seq_count, seq_len, local_heads, HEAD_DIM)
    mixture, log_totals = lax.map(
        lambda element: attend_forward(
            element[0], element[1], element[2], element[3], element[4], block_rows, factor
        ),
        (shaped[0], shaped[1], shaped[2], groups, masks),
    )
    attended = mixture.reshape(seq_count * seq_len, local_heads * HEAD_DIM).astype(jnp.bfloat16)
    resid = latent_rows + settle_rows(
        jnp.einsum("rk,dk->rd", attended, out_rows, preferred_element_type=jnp.float32)
    )
    inputs_c = spread_rows(norm_rows(resid, gains_full[1], offsets_full[1]).astype(jnp.bfloat16))
    upward = jnp.dot(inputs_c, up_rows, preferred_element_type=jnp.float32)
    hidden = jax.nn.gelu(upward).astype(jnp.bfloat16)
    output = resid + settle_rows(
        jnp.einsum("rf,df->rd", hidden, down_rows, preferred_element_type=jnp.float32)
    )
    saved = (inputs_a, shaped, log_totals, attended, resid, inputs_c, upward, hidden)
    return (output, saved)


def backward_pass(latent_rows, grad_rows, weights, saved, groups, masks, block_rows, factor):
    qkv_rows, out_rows, up_rows, down_rows, gains, offsets = weights
    gains_full = gains.astype(jnp.float32)
    offsets_full = offsets.astype(jnp.float32)
    inputs_a, shaped, log_totals, attended, resid, inputs_c, upward, hidden = saved
    seq_count = groups.shape[0]
    seq_len = groups.shape[1]
    local_heads = shaped.shape[3]
    grad_z = spread_rows(grad_rows.astype(jnp.bfloat16))
    grad_down = jnp.einsum("rd,rf->df", grad_z, hidden, preferred_element_type=jnp.float32)
    grad_hidden = jnp.einsum("rd,df->rf", grad_z, down_rows, preferred_element_type=jnp.float32)
    gelu_pull = jax.vjp(jax.nn.gelu, upward)[1]
    grad_upward = gelu_pull(grad_hidden)[0].astype(jnp.bfloat16)
    grad_up = jnp.einsum("rd,rf->df", inputs_c, grad_upward, preferred_element_type=jnp.float32)
    grad_norm_two = settle_rows(
        jnp.einsum("rf,df->rd", grad_upward, up_rows, preferred_element_type=jnp.float32)
    )
    norm_pull_two = jax.vjp(norm_rows, resid, gains_full[1], offsets_full[1])[1]
    resid_part, gain_two, offset_two = norm_pull_two(grad_norm_two)
    grad_resid = grad_rows + resid_part
    grad_branch = spread_rows(grad_resid.astype(jnp.bfloat16))
    grad_out = jnp.einsum("rd,rk->dk", grad_branch, attended, preferred_element_type=jnp.float32)
    grad_attended = jnp.einsum(
        "rd,dk->rk", grad_branch, out_rows, preferred_element_type=jnp.float32
    )
    grad_attended = grad_attended.astype(jnp.bfloat16).reshape(
        seq_count, seq_len, local_heads, HEAD_DIM
    )
    grad_queries, grad_keys, grad_values = lax.map(
        lambda element: attend_backward(
            element[0],
            element[1],
            element[2],
            element[3],
            element[4],
            element[5],
            element[6],
            block_rows,
            factor,
        ),
        (shaped[0], shaped[1], shaped[2], grad_attended, log_totals, groups, masks),
    )
    grad_projected = (
        jnp.stack([grad_queries, grad_keys, grad_values])
        .reshape(3, seq_count * seq_len, local_heads * HEAD_DIM)
        .astype(jnp.bfloat16)
    )
    grad_qkv = jnp.einsum(
        "rd,tre->tde", inputs_a, grad_projected, preferred_element_type=jnp.float32
    )
    grad_norm_one = settle_rows(
        jnp.einsum("tre,tde->rd", grad_projected, qkv_rows, preferred_element_type=jnp.float32)
    )
    norm_pull_one = jax.vjp(norm_rows, latent_rows, gains_full[0], offsets_full[0])[1]
    rows_part, gain_one, offset_one = norm_pull_one(grad_norm_one)
    grad_latents = grad_resid + rows_part
    grad_gains = jnp.stack([gain_one, gain_two])
    grad_offsets = jnp.stack([offset_one, offset_two])
    return (grad_latents, (grad_qkv, grad_out, grad_up, grad_down, grad_gains, grad_offsets))


def add_trees(first_tree, second_tree):
    if first_tree is None:
        return second_tree
    return tuple((left + right for left, right in zip(first_tree, second_tree)))


def body(latents, group_ids, pad_mask, w_qkv, w_out, w_up, w_down, norm_gain, norm_bias, out_grad):
    micro_count = latents.shape[0]
    seq_len = group_ids.shape[2]
    block_rows = min(512, seq_len)
    factor = HEAD_DIM ** (-0.5)
    outputs = []
    input_grads = []
    totals = None
    for batch_index in range(micro_count):
        latent_rows = latents[batch_index]
        groups = group_ids[batch_index]
        masks = pad_mask[batch_index]
        forward_weights = (
            lax.all_gather(w_qkv, "dp", axis=1, tiled=True),
            lax.all_gather(w_out, "dp", axis=0, tiled=True),
            lax.all_gather(w_up, "dp", axis=0, tiled=True),
            lax.all_gather(w_down, "dp", axis=0, tiled=True),
            lax.all_gather(norm_gain, "dp", axis=1, tiled=True),
            lax.all_gather(norm_bias, "dp", axis=1, tiled=True),
        )
        output, saved = forward_pass(
            latent_rows, forward_weights, groups, masks, block_rows, factor
        )
        outputs.append(output)
        backward_weights = (
            lax.all_gather(w_qkv, "dp", axis=1, tiled=True),
            lax.all_gather(w_out, "dp", axis=0, tiled=True),
            lax.all_gather(w_up, "dp", axis=0, tiled=True),
            lax.all_gather(w_down, "dp", axis=0, tiled=True),
            lax.all_gather(norm_gain, "dp", axis=1, tiled=True),
            lax.all_gather(norm_bias, "dp", axis=1, tiled=True),
        )
        grad_latents, partials = backward_pass(
            latent_rows,
            out_grad[batch_index],
            backward_weights,
            saved,
            groups,
            masks,
            block_rows,
            factor,
        )
        input_grads.append(grad_latents)
        norm_sums = lax.psum((partials[4], partials[5]), "mp")
        shares = (
            lax.psum_scatter(partials[0], "dp", scatter_dimension=1, tiled=True),
            lax.psum_scatter(partials[1], "dp", scatter_dimension=0, tiled=True),
            lax.psum_scatter(partials[2], "dp", scatter_dimension=0, tiled=True),
            lax.psum_scatter(partials[3], "dp", scatter_dimension=0, tiled=True),
            lax.psum_scatter(norm_sums[0], "dp", scatter_dimension=1, tiled=True),
            lax.psum_scatter(norm_sums[1], "dp", scatter_dimension=1, tiled=True),
        )
        totals = add_trees(totals, shares)
    return (
        jnp.stack(outputs),
        jnp.stack(input_grads),
        totals[0],
        totals[1],
        totals[2],
        totals[3],
        totals[4],
        totals[5],
    )


def solution(mesh):
    return jax.shard_map(
        body,
        mesh=mesh,
        in_specs=(
            P(None, ("dp", "mp"), None),
            P(None, "dp", None),
            P(None, "dp", None),
            P(None, "dp", "mp"),
            P("dp", "mp"),
            P("dp", "mp"),
            P("dp", "mp"),
            P(None, "dp"),
            P(None, "dp"),
            P(None, ("dp", "mp"), None),
        ),
        out_specs=(
            P(None, ("dp", "mp"), None),
            P(None, ("dp", "mp"), None),
            P(None, "dp", "mp"),
            P("dp", "mp"),
            P("dp", "mp"),
            P("dp", "mp"),
            P(None, "dp"),
            P(None, "dp"),
        ),
        check_vma=False,
    )
```

profile of v0, /device:TPU:0, one launch (start us, length us, event | category | flops | bytes accessed | tf_op | source)
XLA Modules:
  0.0 1899.2 jit_solution(16451634394889164312)
XLA Ops:
  9.2 10.3 all_gather.36
  19.5 8.6 all_gather.37
  35.2 9.0 all_gather.40
  44.2 43.0 %all-gather.16.cloned.1.call-done = bf16[1024,1024]{1,0:T(8,128)(2,1)} async-done(((bf16[256,1024]{1,0:T(8,128)(2,1)}), bf16[1024,1024]{1,0:T(8,128)(2,1)}) %all-gather.16.cloned.1.call-update) | async-done | bytes 2097168 | tf_op jit(solution)/shard_map/all_gather | solution.py:18
  92.1 12.2 while.141
  109.1 24.9 %all-gather.26.cloned.1.call-done = bf16[1024,1024]{1,0:T(8,128)(2,1)} async-done(((bf16[256,1024]{1,0:T(8,128)(2,1)}), bf16[1024,1024]{1,0:T(8,128)(2,1)}) %all-gather.26.cloned.1.call-update) | async-done | bytes 2097168 | tf_op jit(solution)/shard_map/all_gather | solution.py:18
  139.0 12.1 while.142
  155.6 25.4 %all-gather.30.cloned.1.call-done = bf16[1024,1024]{1,0:T(8,128)(2,1)} async-done(((bf16[256,1024]{1,0:T(8,128)(2,1)}), bf16[1024,1024]{1,0:T(8,128)(2,1)}) %all-gather.30.cloned.1.call-update) | async-done | bytes 2097168 | tf_op jit(solution)/shard_map/all_gather | solution.py:18
  185.9 12.1 while.143
  207.2 51.2 %reduce-scatter.23.cloned.1.call-done = f32[256,1024]{1,0:T(8,128)} async-done(((f32[1024,1024]{1,0:T(8,128)}), f32[256,1024]{1,0:T(8,128)}) %reduce-scatter.23.cloned.1.call-update) | async-done | bytes 1048592 | tf_op jit(solution)/shard_map/reduce_scatter | solution.py:22
  258.4 79.6 %reduce-scatter.27.cloned.1.call-done = f32[256,1024]{1,0:T(8,128)} async-done(((f32[1024,1024]{1,0:T(8,128)}), f32[256,1024]{1,0:T(8,128)}) %reduce-scatter.27.cloned.1.call-update) | async-done | bytes 1048592 | tf_op jit(solution)/shard_map/reduce_scatter | solution.py:22
  338.0 79.6 %reduce-scatter.31.cloned.1.call-done = f32[256,1024]{1,0:T(8,128)} async-done(((f32[1024,1024]{1,0:T(8,128)}), f32[256,1024]{1,0:T(8,128)}) %reduce-scatter.31.cloned.1.call-update) | async-done | bytes 1048592 | tf_op jit(solution)/shard_map/reduce_scatter | solution.py:22
  425.2 41.1 %all-gather.38.cloned.1.call-done = bf16[1024,1024]{1,0:T(8,128)(2,1)} async-done(((bf16[256,1024]{1,0:T(8,128)(2,1)}), bf16[1024,1024]{1,0:T(8,128)(2,1)}) %all-gather.38.cloned.1.call-update) | async-done | bytes 2097168 | tf_op jit(solution)/shard_map/all_gather | solution.py:18
  466.3 28.7 %all-gather.24.cloned.1.call-done = bf16[1024,1024]{1,0:T(8,128)(2,1)} async-done(((bf16[128,1024]{1,0:T(8,128)(2,1)}), bf16[1024,1024]{1,0:T(8,128)(2,1)}) %all-gather.24.cloned.1.call-update) | async-done | bytes 2097168 | tf_op jit(solution)/shard_map/all_gather | solution.py:228
  495.0 6.7 fusion.238
  501.6 23.2 %all-gather.22.cloned.1.call-done = bf16[1024,1024]{1,0:T(8,128)(2,1)} async-done(((bf16[128,1024]{1,0:T(8,128)(2,1)}), bf16[1024,1024]{1,0:T(8,128)(2,1)}) %all-gather.22.cloned.1.call-update) | async-done | bytes 2097168 | tf_op jit(solution)/shard_map/all_gather | solution.py:227
  524.8 47.6 %all-gather.28.cloned.1.call-done = bf16[1024,1024]{1,0:T(8,128)(2,1)} async-done(((bf16[256,1024]{1,0:T(8,128)(2,1)}), bf16[1024,1024]{1,0:T(8,128)(2,1)}) %all-gather.28.cloned.1.call-update) | async-done | bytes 2097168 | tf_op jit(solution)/shard_map/all_gather | solution.py:18
  572.4 10.0 fusion.142
  583.7 4.5 fusion.239
  588.7 30.5 %all-gather.34.cloned.1.call-done = bf16[1024,1024]{1,0:T(8,128)(2,1)} async-done(((bf16[256,1024]{1,0:T(8,128)(2,1)}), bf16[1024,1024]{1,0:T(8,128)(2,1)}) %all-gather.34.cloned.1.call-update) | async-done | bytes 2097168 | tf_op jit(solution)/shard_map/all_gather | solution.py:18
  619.2 5.9 fusion.236
  625.1 41.0 %all-gather.20.cloned.1.call-done = bf16[1024,1024]{1,0:T(8,128)(2,1)} async-done(((bf16[256,1024]{1,0:T(8,128)(2,1)}), bf16[1024,1024]{1,0:T(8,128)(2,1)}) %all-gather.20.cloned.1.call-update) | async-done | bytes 2097168 | tf_op jit(solution)/shard_map/all_gather | solution.py:18
  666.1 10.0 fusion.135
  677.4 4.3 fusion.237
  681.9 7.0 fusion.218
  689.1 23.2 %all-gather.42.cloned.1.call-done = bf16[1024,1024]{1,0:T(8,128)(2,1)} async-done(((bf16[256,1024]{1,0:T(8,128)(2,1)}), bf16[1024,1024]{1,0:T(8,128)(2,1)}) %all-gather.42.cloned.1.call-update) | async-done | bytes 2097168 | tf_op jit(solution)/shard_map/all_gather | solution.py:18
  712.3 5.9 fusion.240
  718.1 40.3 %all-gather.32.cloned.1.call-done = bf16[1024,1024]{1,0:T(8,128)(2,1)} async-done(((bf16[256,1024]{1,0:T(8,128)(2,1)}), bf16[1024,1024]{1,0:T(8,128)(2,1)}) %all-gather.32.cloned.1.call-update) | async-done | bytes 2097168 | tf_op jit(solution)/shard_map/all_gather | solution.py:18
  758.4 10.0 fusion.149
  769.8 4.4 fusion.241
  774.2 6.9 fusion.216
  781.2 6.9 fusion.219
  788.4 47.8 %reduce-scatter.39.cloned.1.call-done = f32[256,1024]{1,0:T(8,128)} async-done(((f32[1024,1024]{1,0:T(8,128)}), f32[256,1024]{1,0:T(8,128)}) %reduce-scatter.39.cloned.1.call-update) | async-done | bytes 1048592 | tf_op jit(solution)/shard_map/reduce_scatter | solution.py:22
  836.2 79.4 %reduce-scatter.35.cloned.1.call-done = f32[256,1024]{1,0:T(8,128)} async-done(((f32[1024,1024]{1,0:T(8,128)}), f32[256,1024]{1,0:T(8,128)}) %reduce-scatter.35.cloned.1.call-update) | async-done | bytes 1048592 | tf_op jit(solution)/shard_map/reduce_scatter | solution.py:22
  918.6 76.6 %reduce-scatter.29.cloned.1.call-done = f32[256,1024]{1,0:T(8,128)} async-done(((f32[1024,1024]{1,0:T(8,128)}), f32[256,1024]{1,0:T(8,128)}) %reduce-scatter.29.cloned.1.call-update) | async-done | bytes 1048592 | tf_op jit(solution)/shard_map/reduce_scatter | solution.py:22
  995.2 79.6 %reduce-scatter.43.cloned.1.call-done = f32[256,1024]{1,0:T(8,128)} async-done(((f32[1024,1024]{1,0:T(8,128)}), f32[256,1024]{1,0:T(8,128)}) %reduce-scatter.43.cloned.1.call-update) | async-done | bytes 1048592 | tf_op jit(solution)/shard_map/reduce_scatter | solution.py:22
  1074.8 79.5 %reduce-scatter.25.cloned.1.call-done = f32[256,1024]{1,0:T(8,128)} async-done(((f32[1024,1024]{1,0:T(8,128)}), f32[256,1024]{1,0:T(8,128)}) %reduce-scatter.25.cloned.1.call-update) | async-done | bytes 1048592 | tf_op jit(solution)/shard_map/reduce_scatter | solution.py:22
  1154.3 4.9 fusion.223
  1159.3 74.6 %reduce-scatter.33.cloned.1.call-done = f32[256,1024]{1,0:T(8,128)} async-done(((f32[1024,1024]{1,0:T(8,128)}), f32[256,1024]{1,0:T(8,128)}) %reduce-scatter.33.cloned.1.call-update) | async-done | bytes 1048592 | tf_op jit(solution)/shard_map/reduce_scatter | solution.py:22
  1240.6 45.2 %all-gather.36.cloned.1.call-done = bf16[1024,1024]{1,0:T(8,128)(2,1)} async-done(((bf16[256,1024]{1,0:T(8,128)(2,1)}), bf16[1024,1024]{1,0:T(8,128)(2,1)}) %all-gather.36.cloned.1.call-update) | async-done | bytes 2097168 | tf_op jit(solution)/shard_map/all_gather | solution.py:18
  1289.2 22.6 %while.144 = (s32[]{:T(128)}, f32[1024,2,128]{0,2,1:T(8,128)S(1)}, f32[1024,2,128]{0,2,1:T(8,128)}, bf16[2,512,2,128]{3,1,2,0:T(8,128)(2,1)}, s32[2]{0:T(128)S(1...) while((s32[]{:T(128)}, f32[1024,2,128]{0,2,1:T(8,128)S(1)}, ...), condition=%wide.region_35.36_spmd.clone, body=%wide.region_33.35_spmd.clone.sunk | while | flops 1361445376 | bytes 53526936 | solution.py:105
  1314.8 5.4 convolution_bitcast_fusion.2
  1320.8 11.4 all-gather.44.cloned.1.call-done
  1336.2 22.6 %while.146 = (s32[]{:T(128)}, f32[1024,2,128]{0,2,1:T(8,128)S(1)}, f32[1024,2,128]{0,2,1:T(8,128)}, bf16[2,512,2,128]{3,1,2,0:T(8,128)(2,1)}, s32[2]{0:T(128)S(1...) while((s32[]{:T(128)}, f32[1024,2,128]{0,2,1:T(8,128)S(1)}, ...), condition=%wide.region_53.54_spmd.clone, body=%wide.region_51.53_spmd.clone.sunk | while | flops 1361445376 | bytes 55624116 | solution.py:105
  1363.0 5.5 convolution_bitcast_fusion
  1368.8 10.4 all-gather.40.cloned.1.call-done
  1383.3 22.6 %while.145 = (s32[]{:T(128)}, f32[1024,2,128]{0,2,1:T(8,128)S(1)}, f32[1024,2,128]{0,2,1:T(8,128)}, bf16[2,512,2,128]{3,1,2,0:T(8,128)(2,1)}, s32[2]{0:T(128)S(1...) while((s32[]{:T(128)}, f32[1024,2,128]{0,2,1:T(8,128)S(1)}, ...), condition=%wide.region_44.45_spmd.clone, body=%wide.region_42.44_spmd.clone.sunk | while | flops 1361445376 | bytes 55624116 | solution.py:105
  1408.5 5.2 convolution_bitcast_fusion.1
  1414.0 5.9 fusion.217
  1422.8 5.2 add_bitcast_fusion
  1438.0 6.2 fusion.243
  1444.2 4.5 fusion.242
  1448.7 8.4 reduce-scatter.37.cloned.1.call-done
  1457.1 79.5 %reduce-scatter.45.cloned.1.call-done = f32[256,1024]{1,0:T(8,128)} async-done(((f32[1024,1024]{1,0:T(8,128)}), f32[256,1024]{1,0:T(8,128)}) %reduce-scatter.45.cloned.1.call-update) | async-done | bytes 1048592 | tf_op jit(solution)/shard_map/reduce_scatter | solution.py:22
  1536.6 79.5 %reduce-scatter.41.cloned.1.call-done = f32[256,1024]{1,0:T(8,128)} async-done(((f32[1024,1024]{1,0:T(8,128)}), f32[256,1024]{1,0:T(8,128)}) %reduce-scatter.41.cloned.1.call-update) | async-done | bytes 1048592 | tf_op jit(solution)/shard_map/reduce_scatter | solution.py:22
  1621.4 9.5 add_add_fusion
  1631.0 40.3 %reduce-scatter.53.cloned.1.call-done = f32[128,1024]{0,1:T(8,128)} async-done(((f32[1024,1024]{0,1:T(8,128)}), f32[128,1024]{0,1:T(8,128)}) %reduce-scatter.53.cloned.1.call-update) | async-done | bytes 524304 | tf_op jit(solution)/shard_map/reduce_scatter | solution.py:260
  1673.3 4.1 pad_maximum_fusion
  1682.7 39.2 %reduce-scatter.47.cloned.1.call-done = f32[3,128,256]{1,2,0:T(8,128)} async-done(((f32[3,1024,256]{1,2,0:T(8,128)}), f32[3,128,256]{1,2,0:T(8,128)}) %reduce-scatter.47.cloned.1.call-update) | async-done | bytes 393232 | tf_op jit(solution)/shard_map/reduce_scatter | solution.py:257
  1730.3 28.7 %reduce-scatter.55.cloned.1.call-done = f32[128,2]{1,0:T(8,128)} async-done(((f32[1024,2]{1,0:T(8,128)}), f32[128,2]{1,0:T(8,128)}) %reduce-scatter.55.cloned.1.call-update) | async-done | bytes 1040
  1759.9 36.7 %reduce-scatter.57.cloned.1.call-done = f32[128,2]{1,0:T(8,128)} async-done(((f32[1024,2]{1,0:T(8,128)}), f32[128,2]{1,0:T(8,128)}) %reduce-scatter.57.cloned.1.call-update) | async-done | bytes 1040
  1797.4 12.3 all-reduce
  1809.7 42.1 %reduce-scatter.51.cloned.1.call-done = f32[128,1024]{1,0:T(8,128)} async-done(((f32[1024,1024]{1,0:T(8,128)}), f32[128,1024]{1,0:T(8,128)}) %reduce-scatter.51.cloned.1.call-update) | async-done | bytes 524304 | tf_op jit(solution)/shard_map/reduce_scatter | solution.py:259
  1851.8 40.0 %reduce-scatter.49.cloned.1.call-done = f32[128,256]{1,0:T(8,128)} async-done(((f32[1024,256]{1,0:T(8,128)}), f32[128,256]{1,0:T(8,128)}) %reduce-scatter.49.cloned.1.call-update) | async-done | bytes 131088 | tf_op jit(solution)/shard_map/reduce_scatter | solution.py:258
  (633 shorter events, 204.6 us)
Async XLA Ops:
  7.2 37.0 %all-gather.18.cloned.1.call-start = ((), (), s32[]{:S(2)}) async-start(), calls=%async_computation.19 | async-start | bytes 1769472 | tf_op jit(solution)/shard_map/all_gather | solution.py:225
  9.1 78.1 %all-gather.16.cloned.1.call-start = ((), (), s32[]{:S(2)}) async-start(), calls=%async_computation.18 | async-start | bytes 2621440 | tf_op jit(solution)/shard_map/all_gather | solution.py:18
  33.8 100.3 %all-gather.26.cloned.1.call-start = ((), (), s32[]{:S(2)}) async-start(), calls=%async_computation.25 | async-start | bytes 2621440 | tf_op jit(solution)/shard_map/all_gather | solution.py:18
  34.5 146.5 %all-gather.30.cloned.1.call-start = ((), (), s32[]{:S(2)}) async-start(), calls=%async_computation.29 | async-start | bytes 2621440 | tf_op jit(solution)/shard_map/all_gather | solution.py:18
  35.1 223.3 %reduce-scatter.23.cloned.1.call-start = ((), (), s32[]{:S(2)}) async-start(), calls=%async_computation.20 | async-start | bytes 5242880 | tf_op jit(solution)/shard_map/reduce_scatter | solution.py:22
  44.2 154.5 %copy-start.35 = (bf16[1024,256]{1,0:T(8,128)(2,1)}, bf16[1024,256]{1,0:T(8,128)(2,1)S(1)}, u32[]{:S(2)}) copy-start(bf16[1024,256]{1,0:T(8,128)(2,1)S(1)} %all_gather.40) | copy-start | bytes 1572868
  108.6 229.4 %reduce-scatter.27.cloned.1.call-start = ((), (), s32[]{:S(2)}) async-start(), calls=%async_computation.26 | async-start | bytes 5242880 | tf_op jit(solution)/shard_map/reduce_scatter | solution.py:22
  155.4 262.1 %reduce-scatter.31.cloned.1.call-start = ((), (), s32[]{:S(2)}) async-start(), calls=%async_computation.30 | async-start | bytes 5242880 | tf_op jit(solution)/shard_map/reduce_scatter | solution.py:22
  202.4 215.1 %copy-start.1 = (f32[3,256,1024]{2,1,0:T(8,128)S(1)}, f32[3,256,1024]{2,1,0:T(8,128)}, u32[]{:S(2)}) copy-start(f32[3,256,1024]{2,1,0:T(8,128)} %param.22) | copy-start | bytes 9437188
  202.5 263.8 %all-gather.38.cloned.1.call-start = ((), (), s32[]{:S(2)}) async-start(), calls=%async_computation.37 | async-start | bytes 2621440 | tf_op jit(solution)/shard_map/all_gather | solution.py:18
  205.8 289.2 %all-gather.24.cloned.1.call-start = ((), (), s32[]{:S(2)}) async-start(), calls=%async_computation.23 | async-start | bytes 2359296 | tf_op jit(solution)/shard_map/all_gather | solution.py:228
  206.5 318.3 %all-gather.22.cloned.1.call-start = ((), (), s32[]{:S(2)}) async-start(), calls=%async_computation.22 | async-start | bytes 2359296 | tf_op jit(solution)/shard_map/all_gather | solution.py:227
  207.1 213.7 %copy-start.83 = (f32[1,1024]{1,0:T(1,128)S(1)}, f32[1,1024]{1,0:T(1,128)}, u32[]{:S(2)}) copy-start(f32[1,1024]{1,0:T(1,128)} %get-tuple-element.1096) | copy-start | bytes 12292
  207.1 213.7 %copy-start.107 = (f32[1,1024]{1,0:T(1,128)S(1)}, f32[1,1024]{1,0:T(1,128)}, u32[]{:S(2)}) copy-start(f32[1,1024]{1,0:T(1,128)} %get-tuple-element.1098) | copy-start | bytes 12292
  207.1 365.3 %all-gather.28.cloned.1.call-start = ((), (), s32[]{:S(2)}) async-start(), calls=%async_computation.27 | async-start | bytes 2621440 | tf_op jit(solution)/shard_map/all_gather | solution.py:18
  422.5 196.7 %all-gather.34.cloned.1.call-start = ((), (), s32[]{:S(2)}) async-start(), calls=%async_computation.33 | async-start | bytes 2621440 | tf_op jit(solution)/shard_map/all_gather | solution.py:18
  423.0 243.0 %all-gather.20.cloned.1.call-start = ((), (), s32[]{:S(2)}) async-start(), calls=%async_computation.21 | async-start | bytes 2621440 | tf_op jit(solution)/shard_map/all_gather | solution.py:18
  423.8 288.5 %all-gather.42.cloned.1.call-start = ((), (), s32[]{:S(2)}) async-start(), calls=%async_computation.41 | async-start | bytes 2621440 | tf_op jit(solution)/shard_map/all_gather | solution.py:18
  424.4 334.1 %all-gather.32.cloned.1.call-start = ((), (), s32[]{:S(2)}) async-start(), calls=%async_computation.31 | async-start | bytes 2621440 | tf_op jit(solution)/shard_map/all_gather | solution.py:18
  424.9 411.3 %reduce-scatter.39.cloned.1.call-start = ((), (), s32[]{:S(2)}) async-start(), calls=%async_computation.38 | async-start | bytes 5242880 | tf_op jit(solution)/shard_map/reduce_scatter | solution.py:22
  524.8 58.9 %copy-start.136 = (bf16[1024,1024]{1,0:T(8,128)(2,1)S(1)}, bf16[1024,1024]{1,0:T(8,128)(2,1)}, u32[]{:S(2)}) copy-start(bf16[1024,1024]{1,0:T(8,128)(2,1)} %all-gather.22.cloned.1.call-done) | copy-start | bytes 6291460
  588.2 327.4 %reduce-scatter.35.cloned.1.call-start = ((), (), s32[]{:S(2)}) async-start(), calls=%async_computation.34 | async-start | bytes 5242880 | tf_op jit(solution)/shard_map/reduce_scatter | solution.py:22
  681.8 313.4 %reduce-scatter.29.cloned.1.call-start = ((), (), s32[]{:S(2)}) async-start(), calls=%async_computation.28 | async-start | bytes 5242880 | tf_op jit(solution)/shard_map/reduce_scatter | solution.py:22
  688.8 385.9 %reduce-scatter.43.cloned.1.call-start = ((), (), s32[]{:S(2)}) async-start(), calls=%async_computation.42 | async-start | bytes 5242880 | tf_op jit(solution)/shard_map/reduce_scatter | solution.py:22
  774.2 380.1 %reduce-scatter.25.cloned.1.call-start = ((), (), s32[]{:S(2)}) async-start(), calls=%async_computation.24 | async-start | bytes 5242880 | tf_op jit(solution)/shard_map/reduce_scatter | solution.py:22
  781.2 452.7 %reduce-scatter.33.cloned.1.call-start = ((), (), s32[]{:S(2)}) async-start(), calls=%async_computation.32 | async-start | bytes 5242880 | tf_op jit(solution)/shard_map/reduce_scatter | solution.py:22
  788.1 127.5 %copy-start.18 = (f32[256,1024]{1,0:T(8,128)S(1)}, f32[256,1024]{1,0:T(8,128)}, u32[]{:S(2)}) copy-start(f32[256,1024]{1,0:T(8,128)} %copy-done.17) | copy-start | bytes 3145732
  788.1 127.5 %copy-start.20 = (f32[256,1024]{1,0:T(8,128)S(1)}, f32[256,1024]{1,0:T(8,128)}, u32[]{:S(2)}) copy-start(f32[256,1024]{1,0:T(8,128)} %copy-done.19) | copy-start | bytes 3145732
  788.1 366.2 %copy-start.16 = (f32[256,1024]{1,0:T(8,128)S(1)}, f32[256,1024]{1,0:T(8,128)}, u32[]{:S(2)}) copy-start(f32[256,1024]{1,0:T(8,128)} %copy-done.15) | copy-start | bytes 3145732
  788.1 497.7 %all-gather.36.cloned.1.call-start = ((), (), s32[]{:S(2)}) async-start(), calls=%async_computation.35 | async-start | bytes 2621440 | tf_op jit(solution)/shard_map/all_gather | solution.py:18
  1159.3 78.4 %copy-start.29 = (f32[256,1024]{1,0:T(8,128)S(1)}, f32[256,1024]{1,0:T(8,128)}, u32[]{:S(2)}) copy-start(f32[256,1024]{1,0:T(8,128)} %get-tuple-element.1023) | copy-start | bytes 3145732
  1159.3 78.4 %copy-start.31 = (f32[256,1024]{1,0:T(8,128)S(1)}, f32[256,1024]{1,0:T(8,128)}, u32[]{:S(2)}) copy-start(f32[256,1024]{1,0:T(8,128)} %get-tuple-element.1089) | copy-start | bytes 3145732
  1159.3 77.8 %copy-start.114 = (f32[256]{0:T(256)}, f32[256]{0:T(256)S(1)}, u32[]{:S(2)}) copy-start(f32[256]{0:T(256)S(1)} %negate_multiply_fusion.3) | copy-start | bytes 3076
  1239.1 50.0 %copy-start.6 = (bf16[1024,2,128]{2,0,1:T(8,128)(2,1)S(1)}, bf16[1024,2,128]{2,0,1:T(8,128)(2,1)}, u32[]{:S(2)}) copy-start(bf16[1024,2,128]{2,0,1:T(8,128)(2,1)} %copy-done.5) | copy-start | bytes 1572868
  1239.2 50.0 %copy-start.12 = (bf16[1024,2,128]{2,0,1:T(8,128)(2,1)S(1)}, bf16[1024,2,128]{2,0,1:T(8,128)(2,1)}, u32[]{:S(2)}) copy-start(bf16[1024,2,128]{2,0,1:T(8,128)(2,1)} %copy-done.11) | copy-start | bytes 1572868
  1239.2 50.0 %copy-start.26 = (bf16[1024,2,128]{2,0,1:T(8,128)(2,1)S(1)}, bf16[1024,2,128]{2,0,1:T(8,128)(2,1)}, u32[]{:S(2)}) copy-start(bf16[1024,2,128]{2,0,1:T(8,128)(2,1)} %copy-done.25) | copy-start | bytes 1572868
  1239.2 50.0 %copy-start.56 = (s32[1024]{0:T(1024)S(1)}, s32[1024]{0:T(1024)}, u32[]{:S(2)}) copy-start(s32[1024]{0:T(1024)} %copy-done.55) | copy-start | bytes 12292
  1239.2 50.0 %copy-start.82 = (s32[1024]{0:T(1024)S(1)}, s32[1024]{0:T(1024)}, u32[]{:S(2)}) copy-start(s32[1024]{0:T(1024)} %copy-done.81) | copy-start | bytes 12292
  1239.2 50.0 %copy-start.85 = (f32[2,2,512]{2,1,0:T(2,128)S(1)}, f32[2,2,512]{2,1,0:T(2,128)}, u32[]{:S(2)}) copy-start(f32[2,2,512]{2,1,0:T(2,128)} %copy-done.84) | copy-start | bytes 24580
  1239.2 92.9 %all-gather.44.cloned.1.call-start = ((), (), s32[]{:S(2)}) async-start(), calls=%async_computation.43 | async-start | bytes 2621440 | tf_op jit(solution)/shard_map/all_gather | solution.py:18
  1240.0 139.3 %all-gather.40.cloned.1.call-start = ((), (), s32[]{:S(2)}) async-start(), calls=%async_computation.39 | async-start | bytes 2621440 | tf_op jit(solution)/shard_map/all_gather | solution.py:18
  1240.5 216.6 %reduce-scatter.37.cloned.1.call-start = ((), (), s32[]{:S(2)}) async-start(), calls=%async_computation.36 | async-start | bytes 5242880 | tf_op jit(solution)/shard_map/reduce_scatter | solution.py:22
  1320.3 216.2 %reduce-scatter.45.cloned.1.call-start = ((), (), s32[]{:S(2)}) async-start(), calls=%async_computation.44 | async-start | bytes 5242880 | tf_op jit(solution)/shard_map/reduce_scatter | solution.py:22
  1368.6 247.5 %reduce-scatter.41.cloned.1.call-start = ((), (), s32[]{:S(2)}) async-start(), calls=%async_computation.40 | async-start | bytes 5242880 | tf_op jit(solution)/shard_map/reduce_scatter | solution.py:22
  1413.7 257.6 %reduce-scatter.53.cloned.1.call-start = ((), (), s32[]{:S(2)}) async-start(), calls=%async_computation.48 | async-start | bytes 4718592 | tf_op jit(solution)/shard_map/reduce_scatter | solution.py:260
  1428.1 293.8 %reduce-scatter.47.cloned.1.call-start = ((), (), s32[]{:S(2)}) async-start(), calls=%async_computation.45 | async-start | bytes 3538944 | tf_op jit(solution)/shard_map/reduce_scatter | solution.py:257
  1437.9 321.1 %reduce-scatter.55.cloned.1.call-start = ((), (), s32[]{:S(2)}) async-start(), calls=%async_computation.49 | async-start | bytes 589824
  1444.1 172.0 %copy-start.2 = (f32[3,256,1024]{2,1,0:T(8,128)S(1)}, f32[3,256,1024]{2,1,0:T(8,128)}, u32[]{:S(2)}) copy-start(f32[3,256,1024]{2,1,0:T(8,128)} %param.22) | copy-start | bytes 9437188
  1444.1 172.0 %copy-start.91 = (f32[1,1024]{1,0:T(1,128)S(1)}, f32[1,1024]{1,0:T(1,128)}, u32[]{:S(2)}) copy-start(f32[1,1024]{1,0:T(1,128)} %copy-done.90) | copy-start | bytes 12292
  1444.1 172.0 %copy-start.94 = (f32[256]{0:T(256)S(1)}, f32[256]{0:T(256)}, u32[]{:S(2)}) copy-start(f32[256]{0:T(256)} %copy-done.93) | copy-start | bytes 3076
  1444.1 172.0 %copy-start.96 = (f32[256]{0:T(256)S(1)}, f32[256]{0:T(256)}, u32[]{:S(2)}) copy-start(f32[256]{0:T(256)} %copy-done.95) | copy-start | bytes 3076
  1444.2 172.0 %copy-start.98 = (f32[256]{0:T(256)S(1)}, f32[256]{0:T(256)}, u32[]{:S(2)}) copy-start(f32[256]{0:T(256)} %copy-done.97) | copy-start | bytes 3076
  1444.2 172.0 %copy-start.102 = (f32[256]{0:T(256)S(1)}, f32[256]{0:T(256)}, u32[]{:S(2)}) copy-start(f32[256]{0:T(256)} %copy-done.101) | copy-start | bytes 3076
  1444.2 172.0 %copy-start.104 = (f32[256]{0:T(256)S(1)}, f32[256]{0:T(256)}, u32[]{:S(2)}) copy-start(f32[256]{0:T(256)} %copy-done.103) | copy-start | bytes 3076
  1444.2 172.0 %copy-start.106 = (f32[256]{0:T(256)S(1)}, f32[256]{0:T(256)}, u32[]{:S(2)}) copy-start(f32[256]{0:T(256)} %copy-done.105) | copy-start | bytes 3076
  1448.7 170.1 %copy-start.100 = (f32[1024]{0:T(1024)S(1)}, f32[1024]{0:T(1024)}, u32[]{:S(2)}) copy-start(f32[1024]{0:T(1024)} %get-tuple-element.1092) | copy-start | bytes 12292
  1448.7 170.1 %copy-start.110 = (f32[1024]{0:T(1024)S(1)}, f32[1024]{0:T(1024)}, u32[]{:S(2)}) copy-start(f32[1024]{0:T(1024)} %get-tuple-element.878) | copy-start | bytes 12292
  1448.7 170.1 %copy-start.111 = (f32[1024]{0:T(1024)S(1)}, f32[1024]{0:T(1024)}, u32[]{:S(2)}) copy-start(f32[1024]{0:T(1024)} %get-tuple-element.1095) | copy-start | bytes 12292
  1448.7 171.3 %copy-start.99 = (f32[1024]{0:T(1024)S(1)}, f32[1024]{0:T(1024)}, u32[]{:S(2)}) copy-start(f32[1024]{0:T(1024)} %get-tuple-element.1090) | copy-start | bytes 12292
  1448.7 171.3 %copy-start.108 = (f32[1024]{0:T(1024)S(1)}, f32[1024]{0:T(1024)}, u32[]{:S(2)}) copy-start(f32[1024]{0:T(1024)} %get-tuple-element.885) | copy-start | bytes 12292
  1448.7 171.3 %copy-start.109 = (f32[1024]{0:T(1024)S(1)}, f32[1024]{0:T(1024)}, u32[]{:S(2)}) copy-start(f32[1024]{0:T(1024)} %get-tuple-element.1093) | copy-start | bytes 12292
  1619.9 176.6 %reduce-scatter.57.cloned.1.call-start = ((), (), s32[]{:S(2)}) async-start(), calls=%async_computation.50 | async-start | bytes 589824
  1621.1 230.8 %reduce-scatter.51.cloned.1.call-start = ((), (), s32[]{:S(2)}) async-start(), calls=%async_computation.47 | async-start | bytes 4718592 | tf_op jit(solution)/shard_map/reduce_scatter | solution.py:259
  1631.0 260.8 %reduce-scatter.49.cloned.1.call-start = ((), (), s32[]{:S(2)}) async-start(), calls=%async_computation.46 | async-start | bytes 1179648 | tf_op jit(solution)/shard_map/reduce_scatter | solution.py:258
  (128 other events, 887.0 us)
Sparse Core Ops, SparseCore 0:
  10.5 28.5 all-gather.17
  41.2 45.9 all-gather.15
  89.3 44.6 all-gather.25
  136.0 44.9 all-gather.29
  183.1 75.2 reduce-scatter.22
  260.7 77.2 reduce-scatter.26
  340.3 77.2 reduce-scatter.30
  419.8 46.4 all-gather.37
  468.3 26.5 all-gather.23
  496.8 27.8 all-gather.21
  526.4 45.9 all-gather.27
  574.5 44.6 all-gather.33
  621.4 44.6 all-gather.19
  667.6 44.6 all-gather.41
  713.8 44.6 all-gather.31
  760.7 75.4 reduce-scatter.38
  838.3 77.2 reduce-scatter.34
  917.9 77.2 reduce-scatter.28
  997.5 77.2 reduce-scatter.42
  1077.0 77.2 reduce-scatter.24
  1156.6 77.2 reduce-scatter.32
  1239.3 46.4 all-gather.35
  1287.5 44.6 all-gather.43
  1334.2 44.9 all-gather.39
  1381.6 75.4 reduce-scatter.36
  1459.2 77.2 reduce-scatter.44
  1538.8 77.2 reduce-scatter.40
  1619.4 51.8 reduce-scatter.52
  1675.6 46.2 reduce-scatter.46
  1724.8 34.1 reduce-scatter.54
  1762.4 34.1 reduce-scatter.56
  1800.5 51.3 reduce-scatter.50
  1855.8 36.0 reduce-scatter.48
where the time goes:
time: 1910 us; the launch traced here: 1900 us
  waiting for transfers between devices  1480 us (77%)
  matrix products  225 us (12%)
  other arithmetic  57.3 us (3%)
  local copies, waits for them, and re-layouts  50.2 us (3%)
  blocking collectives  40.2 us (2%)
  loops' own time  20.7 us (1%)
    reduce_scatter x12, waiting for transfers between devices, settle_rows(): return lax.psum_scatter(partial_rows, 'mp', scatter_dimension=0, tiled=True)  815 us
    all_gather x12, waiting for transfers between devices, spread_rows(): return lax.all_gather(rows_local, 'mp', axis=0, tiled=True)  384 us
    unnamed x35, waiting for transfers between devices  71.6 us
    reduce_scatter x1, waiting for transfers between devices, body(): lax.psum_scatter(partials[2], 'dp', scatter_dimension=0, tiled=True)  42.1 us
    reduce_scatter x1, waiting for transfers between devices, body(): lax.psum_scatter(partials[3], 'dp', scatter_dimension=0, tiled=True)  40.3 us
    reduce_scatter x1, waiting for transfers between devices, body(): lax.psum_scatter(partials[1], 'dp', scatter_dimension=0, tiled=True)  40 us
    reduce_scatter x1, waiting for transfers between devices, body(): lax.psum_scatter(partials[0], 'dp', scatter_dimension=1, tiled=True)  39.2 us
  transfers between devices with their start and end apart: 33, of which 32 were waited for; matrix products, arithmetic and copies ran while one was open for 17% of the time, Pallas kernels for 0%

commit v1 on v0

--- a/solution.py
+++ b/solution.py
@@ -5,6 +5,17 @@
 
 HEAD_DIM = 128
 epsilon = 1e-05
+
+
+def gather_around(x, axis, dim):
+    ways = lax.axis_size(axis)
+    pieces = [x]
+    for far in range(1, ways):
+        pieces.append(
+            lax.ppermute(pieces[far - 1], axis, [(d, (d - 1) % ways) for d in range(ways)])
+        )
+    line = jnp.concatenate(pieces, axis=dim)
+    return jnp.roll(line, lax.axis_index(axis) * x.shape[dim], axis=dim)
 
 
 def norm_rows(values, scaling, offset):
@@ -15,7 +26,7 @@
 
 
 def spread_rows(rows_local):
-    return lax.all_gather(rows_local, "mp", axis=0, tiled=True)
+    return gather_around(rows_local, "mp", 0)
 
 
 def settle_rows(partial_rows):

time: 1910 us -> 1840 us (0.963)
  waiting for transfers between devices: 1480 us -> 1240 us
  other arithmetic: 57.3 us -> 180 us
  starting transfers between devices: 4.37 us -> 77.4 us
  matrix products: 225 us -> 198 us
    ppermute x0 -> x36, waiting for transfers between devices: none -> 576 us  [gather_around(): lax.ppermute(pieces[far - 1], axis, [(d, (d - 1) % ways) for d in range(w...]
    all_gather x12 -> x0, waiting for transfers between devices: 384 us -> none  [spread_rows(): return lax.all_gather(rows_local, 'mp', axis=0, tiled=True)]
    reduce_scatter x12, waiting for transfers between devices: 815 us -> 446 us  [settle_rows(): return lax.psum_scatter(partial_rows, 'mp', scatter_dimension=0, tiled=True)]
    concatenate x0 -> x9, other arithmetic: none -> 90.3 us  [gather_around(): return jnp.roll(line, lax.axis_index(axis) * x.shape[dim], axis=dim)]
    ppermute x0 -> x36, starting transfers between devices: none -> 75.8 us  [gather_around(): lax.ppermute(pieces[far - 1], axis, [(d, (d - 1) % ways) for d in range(w...]
    dynamic_slice x0 -> x3, other arithmetic: none -> 34 us  [gather_around(): return jnp.roll(line, lax.axis_index(axis) * x.shape[dim], axis=dim)]
    all_gather x1, waiting for transfers between devices: 28.7 us -> 0.01 us  [body(): lax.all_gather(w_down, 'dp', axis=0, tiled=True)]
    reduce_scatter x1, waiting for transfers between devices: 39.2 us -> 13.3 us  [body(): lax.psum_scatter(partials[0], 'dp', scatter_dimension=1, tiled=True)]
  transfers between devices with their start and end apart: 33 -> 57, of which waited for: 32 -> 44; matrix products, arithmetic and copies ran while one was open for 17% -> 21% of each run, Pallas kernels for 0% -> 0%
where the time goes in v1:
time: 1840 us; the launch traced here: 1830 us
  waiting for transfers between devices  1240 us (67%)
  matrix products  198 us (11%)
  other arithmetic  180 us (10%)
  starting transfers between devices  77.4 us (4%)
  local copies, waits for them, and re-layouts  60.7 us (3%)
  blocking collectives  40 us (2%)
  loops' own time  20.6 us (1%)
    ppermute x36, waiting for transfers between devices, gather_around(): lax.ppermute(pieces[far - 1], axis, [(d, (d - 1) % ways) for d in range(w...  576 us
    reduce_scatter x12, waiting for transfers between devices, settle_rows(): return lax.psum_scatter(partial_rows, 'mp', scatter_dimension=0, tiled=True)  446 us
    concatenate x9, other arithmetic, gather_around(): return jnp.roll(line, lax.axis_index(axis) * x.shape[dim], axis=dim)  90.3 us
    ppermute x36, starting transfers between devices, gather_around(): lax.ppermute(pieces[far - 1], axis, [(d, (d - 1) % ways) for d in range(w...  75.8 us
    unnamed x23, waiting for transfers between devices  66 us
    reduce_scatter x1, waiting for transfers between devices, body(): lax.psum_scatter(partials[2], 'dp', scatter_dimension=0, tiled=True)  55.1 us
    reduce_scatter x1, waiting for transfers between devices, body(): lax.psum_scatter(partials[3], 'dp', scatter_dimension=0, tiled=True)  42.6 us
    reduce_scatter x1, waiting for transfers between devices, body(): lax.psum_scatter(partials[1], 'dp', scatter_dimension=0, tiled=True)  40.1 us
  transfers between devices with their start and end apart: 57, of which 44 were waited for; matrix products, arithmetic and copies ran while one was open for 21% of the time, Pallas kernels for 0%

profile of v1, /device:TPU:0, one launch (start us, length us, event | category | flops | bytes accessed | tf_op | source)
XLA Modules:
  0.0 1833.1 jit_solution(7048826990136755538)
XLA Ops:
  11.9 10.2 all_gather.13
  22.7 8.7 all_gather.12
  38.0 11.7 collective-permute-done
  54.0 10.8 collective-permute-done.1
  69.1 8.9 all_gather.15
  79.1 9.7 fusion.233
  96.9 12.1 while.141
  117.7 21.0 %collective-permute-done.6 = bf16[256,1024]{1,0:T(8,128)(2,1)S(1)} collective-permute-done((bf16[256,1024]{1,0:T(8,128)(2,1)S(1)}, bf16[256,1024]{1,0:T(8,128)(2,1)S(1)}, u32[]{:S(2)}, u32[]{:S(2)}) %collective-permute-start.6) | collective-permute-done | bytes 524320 | tf_op jit(solution)/shard_map/ppermute | solution.py:15
  142.9 31.8 %collective-permute-done.7 = bf16[256,1024]{1,0:T(8,128)(2,1)S(1)} collective-permute-done((bf16[256,1024]{1,0:T(8,128)(2,1)S(1)}, bf16[256,1024]{1,0:T(8,128)(2,1)S(1)}, u32[]{:S(2)}, u32[]{:S(2)}) %collective-permute-start.7) | collective-permute-done | bytes 524320 | tf_op jit(solution)/shard_map/ppermute | solution.py:15
  174.7 40.8 %collective-permute-done.8 = bf16[256,1024]{1,0:T(8,128)(2,1)S(1)} collective-permute-done((bf16[256,1024]{1,0:T(8,128)(2,1)S(1)}, bf16[256,1024]{1,0:T(8,128)(2,1)S(1)}, u32[]{:S(2)}, u32[]{:S(2)}) %collective-permute-start.8) | collective-permute-done | bytes 524320 | tf_op jit(solution)/shard_map/ppermute | solution.py:15
  215.6 11.9 fusion.218
  230.4 12.2 while.142
  247.0 35.7 %collective-permute-done.12 = bf16[256,1024]{1,0:T(8,128)(2,1)S(1)} collective-permute-done((bf16[256,1024]{1,0:T(8,128)(2,1)S(1)}, bf16[256,1024]{1,0:T(8,128)(2,1)S(1)}, u32[]{:S(2)}, u32[]{:S(2)}) %collective-permute-start.12) | collective-permute-done | bytes 524320 | tf_op jit(solution)/shard_map/ppermute | solution.py:15
  282.7 36.1 %collective-permute-done.13 = bf16[256,1024]{1,0:T(8,128)(2,1)S(1)} collective-permute-done((bf16[256,1024]{1,0:T(8,128)(2,1)S(1)}, bf16[256,1024]{1,0:T(8,128)(2,1)S(1)}, u32[]{:S(2)}, u32[]{:S(2)}) %collective-permute-start.13) | collective-permute-done | bytes 524320 | tf_op jit(solution)/shard_map/ppermute | solution.py:15
  318.8 25.8 %collective-permute-done.14 = bf16[256,1024]{1,0:T(8,128)(2,1)S(1)} collective-permute-done((bf16[256,1024]{1,0:T(8,128)(2,1)S(1)}, bf16[256,1024]{1,0:T(8,128)(2,1)S(1)}, u32[]{:S(2)}, u32[]{:S(2)}) %collective-permute-start.14) | collective-permute-done | bytes 524320 | tf_op jit(solution)/shard_map/ppermute | solution.py:15
  344.6 12.3 fusion.203
  359.9 12.3 while.143
  381.4 73.5 %reduce-scatter.31.cloned.1.call-done = f32[256,1024]{1,0:T(8,128)} async-done(((f32[1024,1024]{1,0:T(8,128)}), f32[256,1024]{1,0:T(8,128)}) %reduce-scatter.31.cloned.1.call-update) | async-done | bytes 1048592 | tf_op jit(solution)/shard_map/reduce_scatter | solution.py:33
  463.0 10.5 collective-permute-done.9
  477.8 7.1 collective-permute-done.25
  489.0 7.0 collective-permute-done.10
  500.2 7.0 collective-permute-done.26
  507.2 11.2 fusion.174
  518.4 12.4 fusion.210
  537.5 8.0 fusion.142
  556.7 22.9 %collective-permute-done.18 = bf16[256,1024]{1,0:T(8,128)(2,1)S(1)} collective-permute-done((bf16[256,1024]{1,0:T(8,128)(2,1)S(1)}, bf16[256,1024]{1,0:T(8,128)(2,1)S(1)}, u32[]{:S(2)}, u32[]{:S(2)}) %collective-permute-start.18) | collective-permute-done | bytes 524320 | tf_op jit(solution)/shard_map/ppermute | solution.py:15
  584.0 23.3 %collective-permute-done.3 = bf16[256,1024]{1,0:T(8,128)(2,1)S(1)} collective-permute-done((bf16[256,1024]{1,0:T(8,128)(2,1)S(1)}, bf16[256,1024]{1,0:T(8,128)(2,1)S(1)}, u32[]{:S(2)}, u32[]{:S(2)}) %collective-permute-start.3) | collective-permute-done | bytes 524320 | tf_op jit(solution)/shard_map/ppermute | solution.py:15
  607.3 30.9 %collective-permute-done.19 = bf16[256,1024]{1,0:T(8,128)(2,1)S(1)} collective-permute-done((bf16[256,1024]{1,0:T(8,128)(2,1)S(1)}, bf16[256,1024]{1,0:T(8,128)(2,1)S(1)}, u32[]{:S(2)}, u32[]{:S(2)}) %collective-permute-start.19) | collective-permute-done | bytes 524320 | tf_op jit(solution)/shard_map/ppermute | solution.py:15
  638.2 21.7 %collective-permute-done.4 = bf16[256,1024]{1,0:T(8,128)(2,1)S(1)} collective-permute-done((bf16[256,1024]{1,0:T(8,128)(2,1)S(1)}, bf16[256,1024]{1,0:T(8,128)(2,1)S(1)}, u32[]{:S(2)}, u32[]{:S(2)}) %collective-permute-start.4) | collective-permute-done | bytes 524320 | tf_op jit(solution)/shard_map/ppermute | solution.py:15
  659.9 14.0 collective-permute-done.20
  674.0 11.9 fusion.188
  689.2 12.1 fusion.225
  721.4 7.2 fusion.278
  733.9 30.1 %collective-permute-done.30 = bf16[256,1024]{1,0:T(8,128)(2,1)S(1)} collective-permute-done((bf16[256,1024]{1,0:T(8,128)(2,1)S(1)}, bf16[256,1024]{1,0:T(8,128)(2,1)S(1)}, u32[]{:S(2)}, u32[]{:S(2)}) %collective-permute-start.30) | collective-permute-done | bytes 524320 | tf_op jit(solution)/shard_map/ppermute | solution.py:15
  764.0 30.9 %collective-permute-done.15 = bf16[256,1024]{1,0:T(8,128)(2,1)S(1)} collective-permute-done((bf16[256,1024]{1,0:T(8,128)(2,1)S(1)}, bf16[256,1024]{1,0:T(8,128)(2,1)S(1)}, u32[]{:S(2)}, u32[]{:S(2)}) %collective-permute-start.15) | collective-permute-done | bytes 524320 | tf_op jit(solution)/shard_map/ppermute | solution.py:15
  794.9 22.9 %collective-permute-done.31 = bf16[256,1024]{1,0:T(8,128)(2,1)S(1)} collective-permute-done((bf16[256,1024]{1,0:T(8,128)(2,1)S(1)}, bf16[256,1024]{1,0:T(8,128)(2,1)S(1)}, u32[]{:S(2)}, u32[]{:S(2)}) %collective-permute-start.31) | collective-permute-done | bytes 524320 | tf_op jit(solution)/shard_map/ppermute | solution.py:15
  817.8 14.0 collective-permute-done.16
  831.8 15.4 collective-permute-done.32
  847.2 11.9 fusion.160
  859.2 12.4 fusion.195
  895.9 41.1 %reduce-scatter.29.cloned.1.call-done = f32[256,1024]{1,0:T(8,128)} async-done(((f32[1024,1024]{1,0:T(8,128)}), f32[256,1024]{1,0:T(8,128)}) %reduce-scatter.29.cloned.1.call-update) | async-done | bytes 1048592 | tf_op jit(solution)/shard_map/reduce_scatter | solution.py:33
  937.0 79.4 %reduce-scatter.25.cloned.1.call-done = f32[256,1024]{1,0:T(8,128)} async-done(((f32[1024,1024]{1,0:T(8,128)}), f32[256,1024]{1,0:T(8,128)}) %reduce-scatter.25.cloned.1.call-update) | async-done | bytes 1048592 | tf_op jit(solution)/shard_map/reduce_scatter | solution.py:33
  1016.5 79.7 %reduce-scatter.43.cloned.1.call-done = f32[256,1024]{1,0:T(8,128)} async-done(((f32[1024,1024]{1,0:T(8,128)}), f32[256,1024]{1,0:T(8,128)}) %reduce-scatter.43.cloned.1.call-update) | async-done | bytes 1048592 | tf_op jit(solution)/shard_map/reduce_scatter | solution.py:33
  1101.1 74.5 %reduce-scatter.33.cloned.1.call-done = f32[256,1024]{1,0:T(8,128)} async-done(((f32[1024,1024]{1,0:T(8,128)}), f32[256,1024]{1,0:T(8,128)}) %reduce-scatter.33.cloned.1.call-update) | async-done | bytes 1048592 | tf_op jit(solution)/shard_map/reduce_scatter | solution.py:33
  1183.4 11.4 collective-permute-done.33
  1199.1 12.3 collective-permute-done.34
  1215.8 7.0 collective-permute-done.27
  1227.0 7.0 collective-permute-done.35
  1244.1 22.5 %while.146 = (s32[]{:T(128)}, f32[1024,2,128]{0,2,1:T(8,128)S(1)}, f32[1024,2,128]{0,2,1:T(8,128)}, bf16[2,512,2,128]{3,1,2,0:T(8,128)(2,1)}, s32[2]{0:T(128)S(1...) while((s32[]{:T(128)}, f32[1024,2,128]{0,2,1:T(8,128)S(1)}, ...), condition=%wide.region_53.55_spmd.clone, body=%wide.region_51.54_spmd.clone.sunk | while | flops 1361445376 | bytes 55624116 | solution.py:116
  1280.4 21.3 %collective-permute-done.21 = bf16[256,1024]{1,0:T(8,128)(2,1)} collective-permute-done((bf16[256,1024]{1,0:T(8,128)(2,1)}, bf16[256,1024]{1,0:T(8,128)(2,1)}, u32[]{:S(2)}, u32[]{:S(2)}) %collective-permute-start.21) | collective-permute-done | bytes 524320 | tf_op jit(solution)/shard_map/ppermute | solution.py:15
  1306.1 23.5 %collective-permute-done.29 = bf16[256,1024]{1,0:T(8,128)(2,1)} collective-permute-done((bf16[256,1024]{1,0:T(8,128)(2,1)}, bf16[256,1024]{1,0:T(8,128)(2,1)}, u32[]{:S(2)}, u32[]{:S(2)}) %collective-permute-start.29) | collective-permute-done | bytes 524320 | tf_op jit(solution)/shard_map/ppermute | solution.py:15
  1339.4 22.6 %while.145 = (s32[]{:T(128)}, f32[1024,2,128]{0,2,1:T(8,128)S(1)}, f32[1024,2,128]{0,2,1:T(8,128)}, bf16[2,512,2,128]{3,1,2,0:T(8,128)(2,1)}, s32[2]{0:T(128)S(1...) while((s32[]{:T(128)}, f32[1024,2,128]{0,2,1:T(8,128)S(1)}, ...), condition=%wide.region_44.46_spmd.clone, body=%wide.region_42.45_spmd.clone.sunk | while | flops 1361445376 | bytes 55624116 | solution.py:116
  1371.5 17.9 collective-permute-done.23
  1397.9 22.6 %while.144 = (s32[]{:T(128)}, f32[1024,2,128]{0,2,1:T(8,128)S(1)}, f32[1024,2,128]{0,2,1:T(8,128)}, bf16[2,512,2,128]{3,1,2,0:T(8,128)(2,1)}, s32[2]{0:T(128)S(1...) while((s32[]{:T(128)}, f32[1024,2,128]{0,2,1:T(8,128)S(1)}, ...), condition=%wide.region_35.37_spmd.clone, body=%wide.region_33.36_spmd.clone.sunk | while | flops 1361445376 | bytes 55624116 | solution.py:116
  1452.1 18.6 %reduce-scatter.41.cloned.1.call-done = f32[256,1024]{1,0:T(8,128)} async-done(((f32[1024,1024]{1,0:T(8,128)}), f32[256,1024]{1,0:T(8,128)}) %reduce-scatter.41.cloned.1.call-update) | async-done | bytes 1048592 | tf_op jit(solution)/shard_map/reduce_scatter | solution.py:33
  1470.6 79.5 %reduce-scatter.37.cloned.1.call-done = f32[256,1024]{1,0:T(8,128)} async-done(((f32[1024,1024]{1,0:T(8,128)}), f32[256,1024]{1,0:T(8,128)}) %reduce-scatter.37.cloned.1.call-update) | async-done | bytes 1048592 | tf_op jit(solution)/shard_map/reduce_scatter | solution.py:33
  1555.6 10.2 add_add_fusion
  1587.5 13.3 reduce-scatter.47.cloned.1.call-done
  1609.1 29.0 %reduce-scatter.55.cloned.1.call-done = f32[128,2]{1,0:T(8,128)} async-done(((f32[1024,2]{1,0:T(8,128)}), f32[128,2]{1,0:T(8,128)}) %reduce-scatter.55.cloned.1.call-update) | async-done | bytes 1040
  1639.0 36.1 %reduce-scatter.57.cloned.1.call-done = f32[128,2]{1,0:T(8,128)} async-done(((f32[1024,2]{1,0:T(8,128)}), f32[128,2]{1,0:T(8,128)}) %reduce-scatter.57.cloned.1.call-update) | async-done | bytes 1040
  1676.1 12.2 all-reduce
  1688.3 42.6 %reduce-scatter.53.cloned.1.call-done = f32[128,1024]{1,0:T(8,128)} async-done(((f32[1024,1024]{1,0:T(8,128)}), f32[128,1024]{1,0:T(8,128)}) %reduce-scatter.53.cloned.1.call-update) | async-done | bytes 524304 | tf_op jit(solution)/shard_map/reduce_scatter | solution.py:271
  1730.9 55.1 %reduce-scatter.51.cloned.1.call-done = f32[128,1024]{1,0:T(8,128)} async-done(((f32[1024,1024]{1,0:T(8,128)}), f32[128,1024]{1,0:T(8,128)}) %reduce-scatter.51.cloned.1.call-update) | async-done | bytes 524304 | tf_op jit(solution)/shard_map/reduce_scatter | solution.py:270
  1786.0 40.1 %reduce-scatter.49.cloned.1.call-done = f32[128,256]{1,0:T(8,128)} async-done(((f32[1024,256]{1,0:T(8,128)}), f32[128,256]{1,0:T(8,128)}) %reduce-scatter.49.cloned.1.call-update) | async-done | bytes 131088 | tf_op jit(solution)/shard_map/reduce_scatter | solution.py:269
  (730 shorter events, 389.9 us)
Async XLA Ops:
  7.2 81.6 %all-gather.4.cloned.1.call-start = ((), (), s32[]{:S(2)}) async-start(), calls=%async_computation.18 | async-start | bytes 1769472 | tf_op jit(solution)/shard_map/all_gather | solution.py:236
  9.2 372.2 %reduce-scatter.23.cloned.1.call-start = ((), (), s32[]{:S(2)}) async-start(), calls=%async_computation.19 | async-start | bytes 5242880 | tf_op jit(solution)/shard_map/reduce_scatter | solution.py:33
  34.4 15.3 collective-permute-start
  49.7 15.1 collective-permute-start.1
  64.8 14.2 collective-permute-start.2
  78.0 294.9 %copy-start.35 = (bf16[1024,256]{1,0:T(8,128)(2,1)}, bf16[1024,256]{1,0:T(8,128)(2,1)S(1)}, u32[]{:S(2)}) copy-start(bf16[1024,256]{1,0:T(8,128)(2,1)S(1)} %all_gather.15) | copy-start | bytes 1572868
  109.1 120.4 %copy-start.80 = (s32[1024]{0:T(1024)}, s32[1024]{0:T(1024)S(1)}, u32[]{:S(2)}) copy-start(s32[1024]{0:T(1024)S(1)} %get-tuple-element.1862) | copy-start | bytes 12292
  109.1 120.4 %copy-start.108 = (s32[1024]{0:T(1024)}, s32[1024]{0:T(1024)S(1)}, u32[]{:S(2)}) copy-start(s32[1024]{0:T(1024)S(1)} %get-tuple-element.1918) | copy-start | bytes 12292
  113.3 268.1 %reduce-scatter.27.cloned.1.call-start = ((), (), s32[]{:S(2)}) async-start(), calls=%async_computation.23 | async-start | bytes 5242880 | tf_op jit(solution)/shard_map/reduce_scatter | solution.py:33
  113.4 25.4 %collective-permute-start.6 = (bf16[256,1024]{1,0:T(8,128)(2,1)S(1)}, bf16[256,1024]{1,0:T(8,128)(2,1)S(1)}, u32[]{:S(2)}, u32[]{:S(2)}) collective-permute-start(bf16[256,1024]{1,0:T(8,128)(2,1)S(1)} %copy-done.47), channel_id=1, source_target_pairs={{0,3},{1,0},{2,1},{3,2},{4,7},{5,4},{6,5},{7,6},{8,11},{9,8},{10,9... | collective-permute-start | bytes 1572872 | tf_op jit(solution)/shard_map/ppermute | solution.py:15
  138.8 35.9 %collective-permute-start.7 = (bf16[256,1024]{1,0:T(8,128)(2,1)S(1)}, bf16[256,1024]{1,0:T(8,128)(2,1)S(1)}, u32[]{:S(2)}, u32[]{:S(2)}) collective-permute-start(bf16[256,1024]{1,0:T(8,128)(2,1)S(1)} %collective-permute-done.6), channel_id=1, source_target_pairs={{0,3},{1,0},{2,1},{3,2},{4,7},{5,4},{6,5},{7,6},{8,11},{9,8},{10,9... | collective-permute-start | bytes 1572872 | tf_op jit(solution)/shard_map/ppermute | solution.py:15
  174.7 40.8 %collective-permute-start.8 = (bf16[256,1024]{1,0:T(8,128)(2,1)S(1)}, bf16[256,1024]{1,0:T(8,128)(2,1)S(1)}, u32[]{:S(2)}, u32[]{:S(2)}) collective-permute-start(bf16[256,1024]{1,0:T(8,128)(2,1)S(1)} %collective-permute-done.7), channel_id=1, source_target_pairs={{0,3},{1,0},{2,1},{3,2},{4,7},{5,4},{6,5},{7,6},{8,11},{9,8},{10,9... | collective-permute-start | bytes 1572872 | tf_op jit(solution)/shard_map/ppermute | solution.py:15
  242.6 116.3 %copy-start.82 = (s32[1024]{0:T(1024)}, s32[1024]{0:T(1024)S(1)}, u32[]{:S(2)}) copy-start(s32[1024]{0:T(1024)S(1)} %get-tuple-element.1863) | copy-start | bytes 12292
  246.8 208.1 %reduce-scatter.31.cloned.1.call-start = ((), (), s32[]{:S(2)}) async-start(), calls=%async_computation.25 | async-start | bytes 5242880 | tf_op jit(solution)/shard_map/reduce_scatter | solution.py:33
  246.9 35.8 %collective-permute-start.12 = (bf16[256,1024]{1,0:T(8,128)(2,1)S(1)}, bf16[256,1024]{1,0:T(8,128)(2,1)S(1)}, u32[]{:S(2)}, u32[]{:S(2)}) collective-permute-start(bf16[256,1024]{1,0:T(8,128)(2,1)S(1)} %copy-done.46), channel_id=1, source_target_pairs={{0,3},{1,0},{2,1},{3,2},{4,7},{5,4},{6,5},{7,6},{8,11},{9,8},{10,9... | collective-permute-start | bytes 1572872 | tf_op jit(solution)/shard_map/ppermute | solution.py:15
  282.7 36.2 %collective-permute-start.13 = (bf16[256,1024]{1,0:T(8,128)(2,1)S(1)}, bf16[256,1024]{1,0:T(8,128)(2,1)S(1)}, u32[]{:S(2)}, u32[]{:S(2)}) collective-permute-start(bf16[256,1024]{1,0:T(8,128)(2,1)S(1)} %collective-permute-done.12), channel_id=1, source_target_pairs={{0,3},{1,0},{2,1},{3,2},{4,7},{5,4},{6,5},{7,6},{8,11},{9,8},{10,9... | collective-permute-start | bytes 1572872 | tf_op jit(solution)/shard_map/ppermute | solution.py:15
  318.8 25.8 %collective-permute-start.14 = (bf16[256,1024]{1,0:T(8,128)(2,1)S(1)}, bf16[256,1024]{1,0:T(8,128)(2,1)S(1)}, u32[]{:S(2)}, u32[]{:S(2)}) collective-permute-start(bf16[256,1024]{1,0:T(8,128)(2,1)S(1)} %collective-permute-done.13), channel_id=1, source_target_pairs={{0,3},{1,0},{2,1},{3,2},{4,7},{5,4},{6,5},{7,6},{8,11},{9,8},{10,9... | collective-permute-start | bytes 1572872 | tf_op jit(solution)/shard_map/ppermute | solution.py:15
  376.5 154.3 %all-gather.6.cloned.1.call-start = ((), (), s32[]{:S(2)}) async-start(), calls=%async_computation.20 | async-start | bytes 2359296 | tf_op jit(solution)/shard_map/all_gather | solution.py:238
  377.1 160.4 %all-gather.8.cloned.1.call-start = ((), (), s32[]{:S(2)}) async-start(), calls=%async_computation.21 | async-start | bytes 2359296 | tf_op jit(solution)/shard_map/all_gather | solution.py:239
  381.3 79.9 %collective-permute-start.24 = (bf16[256,1024]{1,0:T(8,128)(2,1)}, bf16[256,1024]{1,0:T(8,128)(2,1)}, u32[]{:S(2)}, u32[]{:S(2)}) collective-permute-start(bf16[256,1024]{1,0:T(8,128)(2,1)} %get-tuple-element.1060), channel_id=1, source_target_pairs={{0,3},{1,0},{2,1},{3,2},{4,7},{5,4},{6,5},{7,6},{8,11},{9,8},{10,9... | collective-permute-start | bytes 1572872 | tf_op jit(solution)/shard_map/ppermute | solution.py:15
  381.3 510.2 %reduce-scatter.39.cloned.1.call-start = ((), (), s32[]{:S(2)}) async-start(), calls=%async_computation.29 | async-start | bytes 5242880 | tf_op jit(solution)/shard_map/reduce_scatter | solution.py:33
  458.6 14.9 collective-permute-start.9
  461.2 23.6 %collective-permute-start.25 = (bf16[256,1024]{1,0:T(8,128)(2,1)}, bf16[256,1024]{1,0:T(8,128)(2,1)S(1)}, u32[]{:S(2)}, u32[]{:S(2)}) collective-permute-start(bf16[256,1024]{1,0:T(8,128)(2,1)} %collective-permute-done.24), channel_id=1, source_target_pairs={{0,3},{1,0},{2,1},{3,2},{4,7},{5,4},{6,5},{7,6},{8,11},{9,8},{10,9... | collective-permute-start | bytes 1572872 | tf_op jit(solution)/shard_map/ppermute | solution.py:15
  473.5 22.5 %collective-permute-start.10 = (bf16[256,1024]{1,0:T(8,128)(2,1)S(1)}, bf16[256,1024]{1,0:T(8,128)(2,1)S(1)}, u32[]{:S(2)}, u32[]{:S(2)}) collective-permute-start(bf16[256,1024]{1,0:T(8,128)(2,1)S(1)} %collective-permute-done.9), channel_id=1, source_target_pairs={{0,3},{1,0},{2,1},{3,2},{4,7},{5,4},{6,5},{7,6},{8,11},{9,8},{10,9... | collective-permute-start | bytes 1572872 | tf_op jit(solution)/shard_map/ppermute | solution.py:15
  484.8 22.4 %collective-permute-start.26 = (bf16[256,1024]{1,0:T(8,128)(2,1)S(1)}, bf16[256,1024]{1,0:T(8,128)(2,1)S(1)}, u32[]{:S(2)}, u32[]{:S(2)}) collective-permute-start(bf16[256,1024]{1,0:T(8,128)(2,1)S(1)} %collective-permute-done.25), channel_id=1, source_target_pairs={{0,3},{1,0},{2,1},{3,2},{4,7},{5,4},{6,5},{7,6},{8,11},{9,8},{10,9... | collective-permute-start | bytes 1572872 | tf_op jit(solution)/shard_map/ppermute | solution.py:15
  495.9 22.4 %collective-permute-start.11 = (bf16[256,1024]{1,0:T(8,128)(2,1)S(1)}, bf16[256,1024]{1,0:T(8,128)(2,1)S(1)}, u32[]{:S(2)}, u32[]{:S(2)}) collective-permute-start(bf16[256,1024]{1,0:T(8,128)(2,1)S(1)} %collective-permute-done.10), channel_id=1, source_target_pairs={{0,3},{1,0},{2,1},{3,2},{4,7},{5,4},{6,5},{7,6},{8,11},{9,8},{10,9... | collective-permute-start | bytes 1572872 | tf_op jit(solution)/shard_map/ppermute | solution.py:15
  551.4 340.2 %reduce-scatter.35.cloned.1.call-start = ((), (), s32[]{:S(2)}) async-start(), calls=%async_computation.27 | async-start | bytes 5242880 | tf_op jit(solution)/shard_map/reduce_scatter | solution.py:33
  552.4 27.2 %collective-permute-start.18 = (bf16[256,1024]{1,0:T(8,128)(2,1)S(1)}, bf16[256,1024]{1,0:T(8,128)(2,1)S(1)}, u32[]{:S(2)}, u32[]{:S(2)}) collective-permute-start(bf16[256,1024]{1,0:T(8,128)(2,1)S(1)} %copy-done.73), channel_id=1, source_target_pairs={{0,3},{1,0},{2,1},{3,2},{4,7},{5,4},{6,5},{7,6},{8,11},{9,8},{10,9... | collective-permute-start | bytes 1572872 | tf_op jit(solution)/shard_map/ppermute | solution.py:15
  556.6 144.7 %copy-start.156 = (bf16[1024,1024]{1,0:T(8,128)(2,1)S(1)}, bf16[1024,1024]{1,0:T(8,128)(2,1)}, u32[]{:S(2)}) copy-start(bf16[1024,1024]{1,0:T(8,128)(2,1)} %all-gather.6.cloned.1.call-done) | copy-start | bytes 6291460
  556.6 50.7 %collective-permute-start.3 = (bf16[256,1024]{1,0:T(8,128)(2,1)S(1)}, bf16[256,1024]{1,0:T(8,128)(2,1)S(1)}, u32[]{:S(2)}, u32[]{:S(2)}) collective-permute-start(bf16[256,1024]{1,0:T(8,128)(2,1)S(1)} %get-tuple-element.1085), channel_id=1, source_target_pairs={{0,3},{1,0},{2,1},{3,2},{4,7},{5,4},{6,5},{7,6},{8,11},{9,8},{10,9... | collective-permute-start | bytes 1572872 | tf_op jit(solution)/shard_map/ppermute | solution.py:15
  579.6 58.6 %collective-permute-start.19 = (bf16[256,1024]{1,0:T(8,128)(2,1)S(1)}, bf16[256,1024]{1,0:T(8,128)(2,1)S(1)}, u32[]{:S(2)}, u32[]{:S(2)}) collective-permute-start(bf16[256,1024]{1,0:T(8,128)(2,1)S(1)} %collective-permute-done.18), channel_id=1, source_target_pairs={{0,3},{1,0},{2,1},{3,2},{4,7},{5,4},{6,5},{7,6},{8,11},{9,8},{10,9... | collective-permute-start | bytes 1572872 | tf_op jit(solution)/shard_map/ppermute | solution.py:15
  607.3 52.6 %collective-permute-start.4 = (bf16[256,1024]{1,0:T(8,128)(2,1)S(1)}, bf16[256,1024]{1,0:T(8,128)(2,1)S(1)}, u32[]{:S(2)}, u32[]{:S(2)}) collective-permute-start(bf16[256,1024]{1,0:T(8,128)(2,1)S(1)} %collective-permute-done.3), channel_id=1, source_target_pairs={{0,3},{1,0},{2,1},{3,2},{4,7},{5,4},{6,5},{7,6},{8,11},{9,8},{10,9... | collective-permute-start | bytes 1572872 | tf_op jit(solution)/shard_map/ppermute | solution.py:15
  638.2 35.7 %collective-permute-start.20 = (bf16[256,1024]{1,0:T(8,128)(2,1)S(1)}, bf16[256,1024]{1,0:T(8,128)(2,1)S(1)}, u32[]{:S(2)}, u32[]{:S(2)}) collective-permute-start(bf16[256,1024]{1,0:T(8,128)(2,1)S(1)} %collective-permute-done.19), channel_id=1, source_target_pairs={{0,3},{1,0},{2,1},{3,2},{4,7},{5,4},{6,5},{7,6},{8,11},{9,8},{10,9... | collective-permute-start | bytes 1572872 | tf_op jit(solution)/shard_map/ppermute | solution.py:15
  659.9 29.3 %collective-permute-start.5 = (bf16[256,1024]{1,0:T(8,128)(2,1)S(1)}, bf16[256,1024]{1,0:T(8,128)(2,1)S(1)}, u32[]{:S(2)}, u32[]{:S(2)}) collective-permute-start(bf16[256,1024]{1,0:T(8,128)(2,1)S(1)} %collective-permute-done.4), channel_id=1, source_target_pairs={{0,3},{1,0},{2,1},{3,2},{4,7},{5,4},{6,5},{7,6},{8,11},{9,8},{10,9... | collective-permute-start | bytes 1572872 | tf_op jit(solution)/shard_map/ppermute | solution.py:15
  714.4 222.6 %reduce-scatter.29.cloned.1.call-start = ((), (), s32[]{:S(2)}) async-start(), calls=%async_computation.24 | async-start | bytes 5242880 | tf_op jit(solution)/shard_map/reduce_scatter | solution.py:33
  721.3 295.1 %reduce-scatter.25.cloned.1.call-start = ((), (), s32[]{:S(2)}) async-start(), calls=%async_computation.22 | async-start | bytes 5242880 | tf_op jit(solution)/shard_map/reduce_scatter | solution.py:33
  728.6 367.6 %reduce-scatter.43.cloned.1.call-start = ((), (), s32[]{:S(2)}) async-start(), calls=%async_computation.31 | async-start | bytes 5242880 | tf_op jit(solution)/shard_map/reduce_scatter | solution.py:33
  729.6 34.4 %collective-permute-start.30 = (bf16[256,1024]{1,0:T(8,128)(2,1)S(1)}, bf16[256,1024]{1,0:T(8,128)(2,1)S(1)}, u32[]{:S(2)}, u32[]{:S(2)}) collective-permute-start(bf16[256,1024]{1,0:T(8,128)(2,1)S(1)} %copy-done.72), channel_id=1, source_target_pairs={{0,3},{1,0},{2,1},{3,2},{4,7},{5,4},{6,5},{7,6},{8,11},{9,8},{10,9... | collective-permute-start | bytes 1572872 | tf_op jit(solution)/shard_map/ppermute | solution.py:15
  733.8 137.7 %copy-start.157 = (bf16[1024,1024]{1,0:T(8,128)(2,1)S(1)}, bf16[1024,1024]{1,0:T(8,128)(2,1)}, u32[]{:S(2)}) copy-start(bf16[1024,1024]{1,0:T(8,128)(2,1)} %all-gather.6.cloned.1.call-done) | copy-start | bytes 6291460
  733.8 61.0 %collective-permute-start.15 = (bf16[256,1024]{1,0:T(8,128)(2,1)S(1)}, bf16[256,1024]{1,0:T(8,128)(2,1)S(1)}, u32[]{:S(2)}, u32[]{:S(2)}) collective-permute-start(bf16[256,1024]{1,0:T(8,128)(2,1)S(1)} %get-tuple-element.1087), channel_id=1, source_target_pairs={{0,3},{1,0},{2,1},{3,2},{4,7},{5,4},{6,5},{7,6},{8,11},{9,8},{10,9... | collective-permute-start | bytes 1572872 | tf_op jit(solution)/shard_map/ppermute | solution.py:15
  764.0 53.8 %collective-permute-start.31 = (bf16[256,1024]{1,0:T(8,128)(2,1)S(1)}, bf16[256,1024]{1,0:T(8,128)(2,1)S(1)}, u32[]{:S(2)}, u32[]{:S(2)}) collective-permute-start(bf16[256,1024]{1,0:T(8,128)(2,1)S(1)} %collective-permute-done.30), channel_id=1, source_target_pairs={{0,3},{1,0},{2,1},{3,2},{4,7},{5,4},{6,5},{7,6},{8,11},{9,8},{10,9... | collective-permute-start | bytes 1572872 | tf_op jit(solution)/shard_map/ppermute | solution.py:15
  794.9 37.0 %collective-permute-start.16 = (bf16[256,1024]{1,0:T(8,128)(2,1)S(1)}, bf16[256,1024]{1,0:T(8,128)(2,1)S(1)}, u32[]{:S(2)}, u32[]{:S(2)}) collective-permute-start(bf16[256,1024]{1,0:T(8,128)(2,1)S(1)} %collective-permute-done.15), channel_id=1, source_target_pairs={{0,3},{1,0},{2,1},{3,2},{4,7},{5,4},{6,5},{7,6},{8,11},{9,8},{10,9... | collective-permute-start | bytes 1572872 | tf_op jit(solution)/shard_map/ppermute | solution.py:15
  817.8 29.5 %collective-permute-start.32 = (bf16[256,1024]{1,0:T(8,128)(2,1)S(1)}, bf16[256,1024]{1,0:T(8,128)(2,1)S(1)}, u32[]{:S(2)}, u32[]{:S(2)}) collective-permute-start(bf16[256,1024]{1,0:T(8,128)(2,1)S(1)} %collective-permute-done.31), channel_id=1, source_target_pairs={{0,3},{1,0},{2,1},{3,2},{4,7},{5,4},{6,5},{7,6},{8,11},{9,8},{10,9... | collective-permute-start | bytes 1572872 | tf_op jit(solution)/shard_map/ppermute | solution.py:15
  831.8 27.4 %collective-permute-start.17 = (bf16[256,1024]{1,0:T(8,128)(2,1)S(1)}, bf16[256,1024]{1,0:T(8,128)(2,1)S(1)}, u32[]{:S(2)}, u32[]{:S(2)}) collective-permute-start(bf16[256,1024]{1,0:T(8,128)(2,1)S(1)} %collective-permute-done.16), channel_id=1, source_target_pairs={{0,3},{1,0},{2,1},{3,2},{4,7},{5,4},{6,5},{7,6},{8,11},{9,8},{10,9... | collective-permute-start | bytes 1572872 | tf_op jit(solution)/shard_map/ppermute | solution.py:15
  884.6 291.0 %reduce-scatter.33.cloned.1.call-start = ((), (), s32[]{:S(2)}) async-start(), calls=%async_computation.26 | async-start | bytes 5242880 | tf_op jit(solution)/shard_map/reduce_scatter | solution.py:33
  891.4 204.7 %copy-start.16 = (f32[256,1024]{1,0:T(8,128)S(1)}, f32[256,1024]{1,0:T(8,128)}, u32[]{:S(2)}) copy-start(f32[256,1024]{1,0:T(8,128)} %copy-done.15) | copy-start | bytes 3145732
  891.4 560.6 %reduce-scatter.45.cloned.1.call-start = ((), (), s32[]{:S(2)}) async-start(), calls=%async_computation.32 | async-start | bytes 5242880 | tf_op jit(solution)/shard_map/reduce_scatter | solution.py:33
  1180.8 14.0 collective-permute-start.33
  1194.8 16.7 collective-permute-start.34
  1199.0 23.7 %collective-permute-start.27 = (bf16[256,1024]{1,0:T(8,128)(2,1)}, bf16[256,1024]{1,0:T(8,128)(2,1)}, u32[]{:S(2)}, u32[]{:S(2)}) collective-permute-start(bf16[256,1024]{1,0:T(8,128)(2,1)} %get-tuple-element.1057), channel_id=1, source_target_pairs={{0,3},{1,0},{2,1},{3,2},{4,7},{5,4},{6,5},{7,6},{8,11},{9,8},{10,9... | collective-permute-start | bytes 1572872 | tf_op jit(solution)/shard_map/ppermute | solution.py:15
  1211.4 22.6 %collective-permute-start.35 = (bf16[256,1024]{1,0:T(8,128)(2,1)}, bf16[256,1024]{1,0:T(8,128)(2,1)}, u32[]{:S(2)}, u32[]{:S(2)}) collective-permute-start(bf16[256,1024]{1,0:T(8,128)(2,1)} %collective-permute-done.34), channel_id=1, source_target_pairs={{0,3},{1,0},{2,1},{3,2},{4,7},{5,4},{6,5},{7,6},{8,11},{9,8},{10,9... | collective-permute-start | bytes 1572872 | tf_op jit(solution)/shard_map/ppermute | solution.py:15
  1222.8 57.2 %collective-permute-start.28 = (bf16[256,1024]{1,0:T(8,128)(2,1)}, bf16[256,1024]{1,0:T(8,128)(2,1)}, u32[]{:S(2)}, u32[]{:S(2)}) collective-permute-start(bf16[256,1024]{1,0:T(8,128)(2,1)} %collective-permute-done.27), channel_id=1, source_target_pairs={{0,3},{1,0},{2,1},{3,2},{4,7},{5,4},{6,5},{7,6},{8,11},{9,8},{10,9... | collective-permute-start | bytes 1572872 | tf_op jit(solution)/shard_map/ppermute | solution.py:15
  1275.5 195.1 %reduce-scatter.41.cloned.1.call-start = ((), (), s32[]{:S(2)}) async-start(), calls=%async_computation.30 | async-start | bytes 5242880 | tf_op jit(solution)/shard_map/reduce_scatter | solution.py:33
  1275.6 26.1 %collective-permute-start.21 = (bf16[256,1024]{1,0:T(8,128)(2,1)}, bf16[256,1024]{1,0:T(8,128)(2,1)}, u32[]{:S(2)}, u32[]{:S(2)}) collective-permute-start(bf16[256,1024]{1,0:T(8,128)(2,1)} %get-tuple-element.1058), channel_id=1, source_target_pairs={{0,3},{1,0},{2,1},{3,2},{4,7},{5,4},{6,5},{7,6},{8,11},{9,8},{10,9... | collective-permute-start | bytes 1572872 | tf_op jit(solution)/shard_map/ppermute | solution.py:15
  1279.9 49.6 %collective-permute-start.29 = (bf16[256,1024]{1,0:T(8,128)(2,1)}, bf16[256,1024]{1,0:T(8,128)(2,1)}, u32[]{:S(2)}, u32[]{:S(2)}) collective-permute-start(bf16[256,1024]{1,0:T(8,128)(2,1)} %collective-permute-done.28), channel_id=1, source_target_pairs={{0,3},{1,0},{2,1},{3,2},{4,7},{5,4},{6,5},{7,6},{8,11},{9,8},{10,9... | collective-permute-start | bytes 1572872 | tf_op jit(solution)/shard_map/ppermute | solution.py:15
  1301.7 69.5 %collective-permute-start.22 = (bf16[256,1024]{1,0:T(8,128)(2,1)}, bf16[256,1024]{1,0:T(8,128)(2,1)}, u32[]{:S(2)}, u32[]{:S(2)}) collective-permute-start(bf16[256,1024]{1,0:T(8,128)(2,1)} %collective-permute-done.21), channel_id=1, source_target_pairs={{0,3},{1,0},{2,1},{3,2},{4,7},{5,4},{6,5},{7,6},{8,11},{9,8},{10,9... | collective-permute-start | bytes 1572872 | tf_op jit(solution)/shard_map/ppermute | solution.py:15
  1371.2 179.0 %reduce-scatter.37.cloned.1.call-start = ((), (), s32[]{:S(2)}) async-start(), calls=%async_computation.28 | async-start | bytes 5242880 | tf_op jit(solution)/shard_map/reduce_scatter | solution.py:33
  1371.2 18.1 collective-permute-start.23
  1429.7 171.1 %reduce-scatter.47.cloned.1.call-start = ((), (), s32[]{:S(2)}) async-start(), calls=%async_computation.33 | async-start | bytes 3538944 | tf_op jit(solution)/shard_map/reduce_scatter | solution.py:268
  1440.4 197.8 %reduce-scatter.55.cloned.1.call-start = ((), (), s32[]{:S(2)}) async-start(), calls=%async_computation.37 | async-start | bytes 589824
  1554.0 121.2 %reduce-scatter.57.cloned.1.call-start = ((), (), s32[]{:S(2)}) async-start(), calls=%async_computation.38 | async-start | bytes 589824
  1555.2 175.7 %reduce-scatter.53.cloned.1.call-start = ((), (), s32[]{:S(2)}) async-start(), calls=%async_computation.36 | async-start | bytes 4718592 | tf_op jit(solution)/shard_map/reduce_scatter | solution.py:271
  1565.9 220.1 %reduce-scatter.51.cloned.1.call-start = ((), (), s32[]{:S(2)}) async-start(), calls=%async_computation.35 | async-start | bytes 4718592 | tf_op jit(solution)/shard_map/reduce_scatter | solution.py:270
  1577.9 248.2 %reduce-scatter.49.cloned.1.call-start = ((), (), s32[]{:S(2)}) async-start(), calls=%async_computation.34 | async-start | bytes 1179648 | tf_op jit(solution)/shard_map/reduce_scatter | solution.py:269
  (177 other events, 4140.7 us)
Sparse Core Ops, SparseCore 0:
  10.5 28.5 all-gather.3
  113.4 104.7 reduce-scatter.22
  246.9 100.0 reduce-scatter.26
  376.6 78.2 reduce-scatter.30
  456.8 27.2 all-gather.5
  486.0 27.8 all-gather.7
  551.5 139.7 reduce-scatter.38
  714.5 137.8 reduce-scatter.34
  854.8 82.1 reduce-scatter.28
  939.1 77.2 reduce-scatter.24
  1018.9 77.2 reduce-scatter.42
  1098.3 77.2 reduce-scatter.32
  1275.6 114.6 reduce-scatter.44
  1392.5 78.0 reduce-scatter.40
  1472.9 77.2 reduce-scatter.36
  1554.0 46.7 reduce-scatter.46
  1604.0 34.0 reduce-scatter.54
  1641.1 34.0 reduce-scatter.56
  1679.5 51.3 reduce-scatter.52
  1734.6 51.2 reduce-scatter.50
  1790.0 36.0 reduce-scatter.48
